TPU v7x, 32 devices: a whole 2x2x4 slice. The times are simulated.
32 devices in a mesh: dp: 16 (over z, y, core), mp: 2 (over x).
Axes of the slice: x: 2, y: 2, z: 4, core: 2. Of those that a mesh axis runs over, the one named last changes fastest.
Arguments:
- tokens: bfloat16 [2048, 2048], P('dp', 'mp'), may hold values from -32 to 32
- lengths: int32 [4], replicated, may hold values from 1 to 1536, 2048 in all
- keep_mask: int32 [2048], replicated, may hold values 0 or 1
- routes: int32 [2048, 8], P('dp'), may hold values from 0 to 63, all different within a row; in each aligned block of 128 rows (0 to 127, 128 to 255, ...) at most 32 rows name the same one
- attention_gain: float32 [2048], replicated, may hold values from 0.1 to 1.9
- mixture_gain: float32 [2048], P('mp'), may hold values from 0.1 to 1.9
- query_gain: float32 [128], replicated, may hold values from 0.5 to 8, as said below
- key_gain: float32 [128], replicated, may hold values from 0.5 to 8, as said below
- query_weight: bfloat16 [2048, 2048], P('dp', 'mp'), may hold values from -0.125 to 0.125
- key_weight: bfloat16 [2048, 2048], P('dp', 'mp'), may hold values from -0.125 to 0.125
- value_weight: bfloat16 [2048, 2048], P('dp', 'mp'), may hold values from -0.125 to 0.125
- output_weight: bfloat16 [2048, 2048], P('mp', 'dp'), may hold values from -0.1875 to 0.1875
- router_weight: float32 [2048, 64], P('mp'), may hold values from -0.125 to 0.125
- expert_gate: bfloat16 [16, 2048, 4096], P('dp', None, 'mp'), may hold values from -0.125 to 0.125
- expert_up: bfloat16 [16, 2048, 4096], P('dp', None, 'mp'), may hold values from -0.125 to 0.125
- expert_down: bfloat16 [16, 4096, 2048], P('dp', 'mp'), may hold values from -0.25 to 0.25
Outputs:
- layer_output: bfloat16 [2048, 2048], P('dp', 'mp')
Inputs may be any that keep to these rules, and one draw needn't show every extreme that they name: The lengths sum to 2048; exactly one is 1536. `routes`: each row names 8 different experts. Within each aligned block of 128 rows (the rows of one index of dp) no expert is named by more than 32 rows, a bound that some block reaches. `query_gain`: Positive. `key_gain`: Positive.
All inputs are finite; a program needn't handle non-finite values.
Results may differ from a plain program's by a relative error of at most 0.012.
The roundings to bfloat16 on the way count: a program that leaves them out, or rounds other values in their place, can miss the bound.
Values may be sent and summed in bfloat16 or wider, within the bound.
A program may use at most 128 MiB of HBM per device.

v0:
```python
import jax
import jax.numpy as jnp
from jax import lax
from jax.sharding import PartitionSpec as P

D = 2048
HEAD_DIM = 128
FF = 1024
EXPERTS = 64
TOPK = 8
CAP = 32
EPS = 1e-06
ROPE_BASE = 10000.0
NEG = -1e30


def rope_tables(position):
    halves = HEAD_DIM // 2
    exponent = jnp.arange(halves, dtype=jnp.float32) * (2.0 / HEAD_DIM)
    frequency = jnp.power(jnp.float32(ROPE_BASE), -exponent)
    angle = position.astype(jnp.float32)[:, None] * frequency[None, :]
    cos_table = jnp.cos(angle)
    sin_table = jnp.sin(angle)
    return (jnp.concatenate([cos_table, cos_table], 1), jnp.concatenate([sin_table, sin_table], 1))


def head_prep(projected, head_gain, cos_table, sin_table):
    row_count = projected.shape[0]
    per_head = projected.reshape(row_count, -1, HEAD_DIM)
    normed = (
        per_head * lax.rsqrt(jnp.mean(per_head * per_head, axis=2, keepdims=True) + EPS) * head_gain
    )
    halves = HEAD_DIM // 2
    rotated = jnp.concatenate([-normed[:, :, halves:], normed[:, :, :halves]], 2)
    turned = normed * cos_table[:, None, :] + rotated * sin_table[:, None, :]
    return turned.reshape(row_count, -1).astype(jnp.bfloat16)


def segment_info(lengths, global_row):
    request_end = jnp.cumsum(lengths)
    request_start = request_end - lengths
    segment = jnp.sum((request_end[None, :] <= global_row[:, None]).astype(jnp.int32), axis=1)
    chosen = segment[:, None] == jnp.arange(lengths.shape[0], dtype=jnp.int32)[None, :]
    begin = jnp.sum(jnp.where(chosen, request_start[None, :], 0), axis=1)
    return (segment, global_row - begin)


def gather_tokens(block):
    return lax.all_gather(block, "dp", axis=0, tiled=True)


def attention(queries, keys, values, query_seg, query_row, key_seg, key_row, keep_mask):
    scale = HEAD_DIM ** (-0.5)
    scores = (
        lax.dot_general(queries, keys, (((1,), (1,)), ((), ())), preferred_element_type=jnp.float32)
        * scale
    )
    visible = (query_seg[:, None] == key_seg[None, :]) & (
        (keep_mask[None, :] == 1) | (query_row[:, None] == key_row[None, :])
    )
    masked = jnp.where(visible, scores, NEG)
    top = jnp.max(masked, axis=1, keepdims=True)
    weights = jnp.where(visible, jnp.exp(masked - top), 0.0)
    totals = jnp.sum(weights, axis=1, keepdims=True)
    mixed = jnp.dot(weights.astype(jnp.bfloat16), values, preferred_element_type=jnp.float32)
    return (mixed / totals).astype(jnp.bfloat16)


def local(
    tokens,
    lengths,
    keep_mask,
    routes,
    attention_gain,
    mixture_gain,
    query_gain,
    key_gain,
    query_weight,
    key_weight,
    value_weight,
    output_weight,
    router_weight,
    expert_gate,
    expert_up,
    expert_down,
):
    tok_rows = tokens.shape[0]
    dp_count = lax.axis_size("dp")
    dp_index = lax.axis_index("dp")
    mp_index = lax.axis_index("mp")
    local_width = query_weight.shape[1]
    local_heads = local_width // HEAD_DIM
    share = dp_count // local_heads
    part = dp_index % share
    total_rows = tok_rows * dp_count
    weight_rows = query_weight.shape[0]
    packed = jnp.stack([query_weight, key_weight, value_weight]).reshape(
        3, weight_rows, local_heads, HEAD_DIM
    )
    packed = packed.transpose(2, 1, 0, 3).reshape(local_heads, weight_rows, 3 * HEAD_DIM)
    packed = jnp.repeat(packed, share, axis=0)
    head_weight = lax.all_to_all(packed, "dp", split_axis=0, concat_axis=0, tiled=True)
    head_weight = head_weight.reshape(dp_count * weight_rows, 3 * HEAD_DIM)
    full_tokens = lax.all_gather(tokens, "mp", axis=1, tiled=True)
    xfloat = full_tokens.astype(jnp.float32)
    normed_in = (
        xfloat * lax.rsqrt(jnp.mean(xfloat * xfloat, axis=1, keepdims=True) + EPS) * attention_gain
    ).astype(jnp.bfloat16)
    all_in = gather_tokens(normed_in)
    all_output_weight = lax.all_gather(output_weight, "dp", axis=1, tiled=True)
    key_row = jnp.arange(total_rows, dtype=jnp.int32)
    key_seg, key_pos = segment_info(lengths, key_row)
    cos_table, sin_table = rope_tables(key_pos)

    def own(array):
        split = array.reshape((local_heads, share, tok_rows) + array.shape[1:])
        taken = lax.dynamic_index_in_dim(split, part, 1, keepdims=False)
        return taken.reshape((local_heads * tok_rows,) + array.shape[1:])

    projected = jnp.dot(all_in, head_weight, preferred_element_type=jnp.float32)
    queries = head_prep(own(projected[:, :HEAD_DIM]), query_gain, own(cos_table), own(sin_table))
    keys = head_prep(projected[:, HEAD_DIM : 2 * HEAD_DIM], key_gain, cos_table, sin_table)
    values = projected[:, 2 * HEAD_DIM :].astype(jnp.bfloat16)
    attended = attention(
        queries, keys, values, own(key_seg), own(key_row), key_seg, key_row, keep_mask
    )
    groups = [[head * share + p for head in range(local_heads)] for p in range(share)]
    attended = lax.all_to_all(
        attended.reshape(local_heads, tok_rows, HEAD_DIM),
        "dp",
        split_axis=0,
        concat_axis=0,
        tiled=True,
        axis_index_groups=groups,
    )
    attended = attended.transpose(1, 0, 2).reshape(tok_rows, local_width)
    partial_out = jnp.dot(attended, all_output_weight, preferred_element_type=jnp.float32)
    summed_out = lax.psum_scatter(partial_out, "mp", scatter_dimension=1, tiled=True)
    residual = (tokens.astype(jnp.float32) + summed_out).astype(jnp.bfloat16)
    hfloat = residual.astype(jnp.float32)
    scaled = hfloat * mixture_gain
    partial_logits = jnp.dot(scaled, router_weight, precision=lax.Precision.HIGHEST)
    square_sum, logit_sum = lax.psum((jnp.sum(hfloat * hfloat, axis=1), partial_logits), "mp")
    inverse = lax.rsqrt(square_sum / D + EPS)[:, None]
    mixed_in = (scaled * inverse).astype(jnp.bfloat16)
    logits = logit_sum * inverse
    experts = jnp.arange(EXPERTS, dtype=jnp.int32)
    named = jnp.any(routes[None, :, :] == experts[:, None, None], axis=2)
    named_float = named.astype(jnp.float32)
    sigmoid_vals = jax.nn.sigmoid(logits).T * named_float
    route_weight = sigmoid_vals / jnp.sum(sigmoid_vals, axis=0, keepdims=True)
    ids = jnp.arange(tok_rows, dtype=jnp.int32)
    earlier = (ids[:, None] < ids[None, :]).astype(jnp.bfloat16)
    before = jnp.dot(named.astype(jnp.bfloat16), earlier, preferred_element_type=jnp.float32)
    place = jnp.where(named, before.astype(jnp.int32), -1)
    exp_local = EXPERTS // dp_count
    gate_local = expert_gate[0]
    up_local = expert_up[0]
    down_local = expert_down[0]
    unit_count = gate_local.shape[1]
    held = max(1, unit_count // FF)
    units = unit_count // held
    first_expert = mp_index * unit_count // FF

    def mine(table):
        split = table.reshape(dp_count, exp_local, tok_rows)
        return lax.dynamic_slice_in_dim(split, first_expert, held, 1)

    slots = jnp.arange(CAP, dtype=jnp.int32)
    chosen = mine(place)[:, :, None, :] == slots[None, None, :, None]
    select = chosen.astype(jnp.bfloat16).reshape(dp_count * held * CAP, tok_rows)
    full_in = lax.all_gather(mixed_in, "mp", axis=1, tiled=True)
    sending = jnp.dot(select, full_in, preferred_element_type=jnp.float32).astype(jnp.bfloat16)
    rows_in = lax.all_to_all(
        sending.reshape(dp_count, held, CAP, D), "dp", split_axis=0, concat_axis=0, tiled=True
    )
    outs = []
    for index in range(held):
        rows = rows_in[:, index].reshape(dp_count * CAP, D)
        low, high = (index * units, (index + 1) * units)
        gate_val = jnp.dot(rows, gate_local[:, low:high], preferred_element_type=jnp.float32)
        up_val = jnp.dot(rows, up_local[:, low:high], preferred_element_type=jnp.float32)
        hidden = (jax.nn.silu(gate_val) * up_val).astype(jnp.bfloat16)
        out = jnp.dot(hidden, down_local[low:high], preferred_element_type=jnp.float32)
        outs.append(out.astype(jnp.bfloat16).reshape(dp_count, CAP, D))
    returned = lax.all_to_all(
        jnp.stack(outs, axis=1), "dp", split_axis=0, concat_axis=0, tiled=True
    ).reshape(dp_count * held * CAP, D)
    spread = jnp.where(chosen, mine(route_weight)[:, :, None, :], 0.0)
    spread = spread.reshape(dp_count * held * CAP, tok_rows)
    spread_high = spread.astype(jnp.bfloat16)
    spread_mid = (spread - spread_high.astype(jnp.float32)).astype(jnp.bfloat16)
    contract = (((0,), (0,)), ((), ()))
    mixture = lax.dot_general(
        spread_high, returned, contract, preferred_element_type=jnp.float32
    ) + lax.dot_general(spread_mid, returned, contract, preferred_element_type=jnp.float32)
    mixture = lax.psum_scatter(mixture, "mp", scatter_dimension=1, tiled=True)
    return (hfloat + mixture).astype(jnp.bfloat16)


def solution(mesh):
    return jax.shard_map(
        local,
        mesh=mesh,
        in_specs=(
            P("dp", "mp"),
            P(),
            P(),
            P("dp", None),
            P(),
            P("mp"),
            P(),
            P(),
            P("dp", "mp"),
            P("dp", "mp"),
            P("dp", "mp"),
            P("mp", "dp"),
            P("mp", None),
            P("dp", None, "mp"),
            P("dp", None, "mp"),
            P("dp", "mp", None),
        ),
        out_specs=P("dp", "mp"),
        check_vma=False,
    )
```

profile of v0, /device:TPU:0, one launch (start us, length us, event | category | flops | bytes accessed | tf_op | source)
XLA Modules:
  0.0 488.3 jit_solution(367880626133548728)
XLA Ops:
  6.5 10.3 %all_gather.12 = bf16[128,2048]{1,0:T(8,128)(2,1)S(1)} all-gather(bf16[128,1024]{1,0:T(8,128)(2,1)} %param.16), channel_id=1, replica_groups=mesh['dp'=16,'mp'=2] {'mp'}, dimensions={1}, use_global_device_ids=true | all-gather | bytes 786432 | tf_op jit(solution)/shard_map/all_gather | solution.py:104
  24.0 6.2 %all-to-all-start = ((bf16[16,128,384]{2,1,0:T(8,128)(2,1)}), bf16[16,128,384]{2,1,0:T(8,128)(2,1)}, u32[]{:S(2)}, u32[]{:S(2)}) async-start(bf16[16,128,384]{2,1,0:T(8,128)(2,1)} %bitcast.10), calls=%async_computation | async-start | bytes 3145728 | tf_op jit(solution)/shard_map/all_to_all | solution.py:102
  31.5 3.7 multiply_cosine_fusion
  38.4 39.1 %all-to-all-done = bf16[16,128,384]{2,1,0:T(8,128)(2,1)} async-done(((bf16[16,128,384]{2,1,0:T(8,128)(2,1)}), bf16[16,128,384]{2,1,0:T(8,128)(2,1)}, u32[]{:S(2)}, u32[]{:S(2)}) %all-to-all-start) | async-done | bytes 1572896 | tf_op jit(solution)/shard_map/all_to_all | solution.py:102
  77.6 43.2 %all-gather.3.cloned.1.call-done = bf16[2048,2048]{1,0:T(8,128)(2,1)} async-done(((bf16[128,2048]{1,0:T(8,128)(2,1)}), bf16[2048,2048]{1,0:T(8,128)(2,1)}) %all-gather.3.cloned.1.call-update) | async-done | bytes 8388624 | tf_op jit(solution)/shard_map/all_gather | solution.py:49
  120.7 6.4 %fusion.88 = f32[2048,384]{0,1:T(8,128)S(1)} fusion(bf16[2048,2048]{1,0:T(8,128)(2,1)} %all-gather.3.cloned.1.call-done, bf16[2048,384]{1,0:T(8,128)(2,1)} %bitcast.11), kind=kOutput, calls=%fused_computation.130 | convolution fusion | flops 3221225472 | bytes 13107200 | tf_op jit(solution)/shard_map/dot_general | solution.py:120
  140.1 5.0 %fusion.3 = f32[1024]{0:T(1024)S(1)} fusion(f32[1024,2048]{1,0:T(8,128)S(1)} %get-tuple-element.24, f32[1024]{0:T(1024)S(1)} %get-tuple-element.23, s32[1024]{0:T(1024)S(1)} %bitcast.112, pred[2048]{0:T(1024)(128)(4,1)S(1)} %broadcast_compare_fusion, s32[2048]{0:T(1024)S(1)} %convert_reduce_fusion, s32[1024]{0:T(1024)S(1)} %bitcast.115), kind=kLoop, calls=%fused_computation.6 | loop fusion | flops 18873344 | bytes 8415232 | tf_op jit(solution)/shard_map/reduce_sum | solution.py:64
  145.0 3.9 fusion.45
  149.8 3.5 all-to-all-start.1
  153.4 24.8 %all-gather.5.cloned.1.call-done = bf16[1024,2048]{1,0:T(8,128)(2,1)} async-done(((bf16[1024,128]{1,0:T(8,128)(2,1)}), bf16[1024,2048]{1,0:T(8,128)(2,1)}) %all-gather.5.cloned.1.call-update) | async-done | bytes 4194320 | tf_op jit(solution)/shard_map/all_gather | solution.py:110
  178.2 3.9 fusion.89
  182.7 20.2 %reduce-scatter.3.cloned.1.call-done = f32[128,1024]{1,0:T(8,128)} async-done(((f32[128,2048]{1,0:T(8,128)}), f32[128,1024]{1,0:T(8,128)}) %reduce-scatter.3.cloned.1.call-update) | async-done | bytes 524304 | tf_op jit(solution)/shard_map/reduce_scatter | solution.py:138
  204.8 7.3 %all-reduce = (f32[128]{0:T(128)S(1)}, f32[128,64]{0,1:T(8,128)S(1)}) all-reduce(f32[128]{0:T(128)S(1)} %get-tuple-element.7, f32[128,64]{0,1:T(8,128)S(1)} %fusion.50), channel_id=1, replica_groups=mesh['dp'=16,'mp'=2] {'mp'}, use_global_device_ids=true, to_apply=%region_12.13 | all-reduce | flops 8320 | bytes 66560 | tf_op jit(solution)/shard_map/psum | solution.py:143
  212.2 7.0 %all_gather.15 = bf16[128,2048]{1,0:T(8,128)(2,1)S(1)} all-gather(bf16[128,1024]{1,0:T(8,128)(2,1)S(1)} %fusion.51), channel_id=1, replica_groups=mesh['dp'=16,'mp'=2] {'mp'}, dimensions={1}, use_global_device_ids=true | all-gather | bytes 786432 | tf_op jit(solution)/shard_map/all_gather | solution.py:172
  220.5 98.4 %all_to_all.20 = bf16[16,2,32,2048]{3,2,1,0:T(8,128)(2,1)S(1)} all-to-all(bf16[16,2,32,2048]{3,2,1,0:T(8,128)(2,1)S(1)} %bitcast.92), channel_id=1, replica_groups=mesh['dp'=16,'mp'=2] {'dp'}, dimensions={0} | all-to-all | bytes 8388608 | tf_op jit(solution)/shard_map/all_to_all | solution.py:174
  321.9 3.7 fusion.11
  325.6 3.7 fusion.7
  329.3 10.5 %fusion.21 = bf16[512,2048]{1,0:T(8,128)(2,1)} fusion(bf16[1,2048,2048]{2,1,0:T(8,128)(2,1)} %param.31, f32[512,1024]{1,0:T(8,128)} %fusion.11, bf16[512,2048]{1,0:T(8,128)(2,1)} %bitcast.99, bf16[2048,2048]{1,0:T(8,128)(2,1)} %bitcast.123), kind=kOutput, calls=%fused_computation.25 | convolution fusion | flops 4299161600 | bytes 14680064 | tf_op jit(solution)/shard_map/dot_general | solution.py:184
  339.9 9.9 %fusion.24 = bf16[512,2048]{1,0:T(8,128)(2,1)} fusion(bf16[1,2048,2048]{2,1,0:T(8,128)(2,1)} %param.31, f32[512,1024]{1,0:T(8,128)} %fusion.7, bf16[512,2048]{1,0:T(8,128)(2,1)S(1)} %bitcast.97, bf16[2048,2048]{1,0:T(8,128)(2,1)} %bitcast.124), kind=kOutput, calls=%fused_computation.26 | convolution fusion | flops 4299161600 | bytes 14680064 | tf_op jit(solution)/shard_map/dot_general | solution.py:184
  349.8 4.6 pad_maximum_fusion
  354.4 5.3 %all-to-all-start.3 = ((bf16[16,2,32,2048]{3,2,1,0:T(8,128)(2,1)}), bf16[16,2,32,2048]{3,2,1,0:T(8,128)(2,1)}, u32[]{:S(2)}, u32[]{:S(2)}) async-start(bf16[16,2,32,2048]{3,2,1,0:T(8,128)(2,1)} %pad_maximum_fusion), calls=%async_computation.4 | async-start | bytes 8388608 | tf_op jit(solution)/shard_map/all_to_all | solution.py:186
  359.9 77.5 %all-to-all-done.3 = bf16[16,2,32,2048]{3,2,1,0:T(8,128)(2,1)} async-done(((bf16[16,2,32,2048]{3,2,1,0:T(8,128)(2,1)}), bf16[16,2,32,2048]{3,2,1,0:T(8,128)(2,1)}, u32[]{:S(2)}, u32[]{:S(2)}) %all-to-all-start.3) | async-done | bytes 4194336 | tf_op jit(solution)/shard_map/all_to_all | solution.py:186
  440.4 3.9 fusion.27
  444.3 35.4 %reduce-scatter.5.cloned.1.call-done = f32[128,1024]{1,0:T(8,128)} async-done(((f32[128,2048]{1,0:T(8,128)}), f32[128,1024]{1,0:T(8,128)}) %reduce-scatter.5.cloned.1.call-update) | async-done | bytes 524304 | tf_op jit(solution)/shard_map/reduce_scatter | solution.py:197
  (96 shorter events, 36.9 us)
Async XLA Ops:
  6.5 197.6 %copy-start = (f32[1024,64]{0,1:T(8,128)S(1)}, f32[1024,64]{0,1:T(8,128)}, u32[]{:S(2)}) copy-start(f32[1024,64]{0,1:T(8,128)} %param.28) | copy-start | bytes 786436
  6.5 114.2 %all-gather.3.cloned.1.call-start = ((), (), s32[]{:S(2)}) async-start(), calls=%async_computation.6 | async-start | bytes 8912896 | tf_op jit(solution)/shard_map/all_gather | solution.py:49
  22.1 8.8 %copy-start.14 = (s32[4]{0:T(128)S(1)}, s32[4]{0:T(128)}, u32[]{:S(2)}) copy-start(s32[4]{0:T(128)} %param.17) | copy-start | bytes 52
  22.1 9.3 %copy-start.10 = (s32[2048]{0:T(1024)S(1)}, s32[2048]{0:T(1024)}, u32[]{:S(2)}) copy-start(s32[2048]{0:T(1024)} %param.18) | copy-start | bytes 24580
  24.0 53.6 %all-to-all-start = ((bf16[16,128,384]{2,1,0:T(8,128)(2,1)}), bf16[16,128,384]{2,1,0:T(8,128)(2,1)}, u32[]{:S(2)}, u32[]{:S(2)}) async-start(bf16[16,128,384]{2,1,0:T(8,128)(2,1)} %bitcast.10), calls=%async_computation | async-start | bytes 3145728 | tf_op jit(solution)/shard_map/all_to_all | solution.py:102
  30.2 148.0 %all-gather.5.cloned.1.call-start = ((), (), s32[]{:S(2)}) async-start(), calls=%async_computation.7 | async-start | bytes 4456448 | tf_op jit(solution)/shard_map/all_gather | solution.py:110
  120.7 8.0 %copy-start.13 = (f32[128]{0:T(128)S(1)}, f32[128]{0:T(128)}, u32[]{:S(2)}) copy-start(f32[128]{0:T(128)} %param.23) | copy-start | bytes 1540
  127.1 1.7 copy-start.3
  128.8 5.4 %copy-start.12 = (f32[128]{0:T(128)S(1)}, f32[128]{0:T(128)}, u32[]{:S(2)}) copy-start(f32[128]{0:T(128)} %param.22) | copy-start | bytes 1540
  134.0 1.3 copy-start.2
  134.4 2.0 copy-start.4
  134.4 2.1 copy-start.7
  134.4 2.2 copy-start.8
  148.9 33.4 %copy-start.11 = (s32[128,8]{0,1:T(8,128)S(1)}, s32[128,8]{0,1:T(8,128)}, u32[]{:S(2)}) copy-start(s32[128,8]{0,1:T(8,128)} %param.19) | copy-start | bytes 12292
  148.9 54.0 %copy-start.6 = (bf16[128,1024]{1,0:T(8,128)(2,1)S(1)}, bf16[128,1024]{1,0:T(8,128)(2,1)}, u32[]{:S(2)}) copy-start(bf16[128,1024]{1,0:T(8,128)(2,1)} %param.16) | copy-start | bytes 786436
  149.8 54.4 %copy-start.9 = (f32[1024]{0:T(1024)S(1)}, f32[1024]{0:T(1024)}, u32[]{:S(2)}) copy-start(f32[1024]{0:T(1024)} %param.21) | copy-start | bytes 12292
  149.8 28.4 %all-to-all-start.1 = ((bf16[8,128,128]{1,2,0:T(8,128)(2,1)}), bf16[8,128,128]{1,2,0:T(8,128)(2,1)S(1)}, u32[]{:S(2)}, u32[]{:S(2)}) async-start(bf16[8,128,128]{1,2,0:T(8,128)(2,1)} %copy.45), calls=%async_computation.1 | async-start | bytes 524288 | tf_op jit(solution)/shard_map/all_to_all | solution.py:128
  153.3 49.6 %reduce-scatter.3.cloned.1.call-start = ((), (), s32[]{:S(2)}) async-start(), calls=%async_computation.8 | async-start | bytes 1572864 | tf_op jit(solution)/shard_map/reduce_scatter | solution.py:138
  220.5 98.9 %slice-start = ((s8[8388608]{0:T(1024)(128)(4,1)}), s8[4194304]{0:T(1024)(128)(4,1)S(1)}, s32[]{:S(2)}) async-start(s8[8388608]{0:T(1024)(128)(4,1)} %bitcast.119), calls=%async_computation.10 | async-start | bytes 8388608
  318.9 2.9 slice-start.1
  319.4 6.2 %copy-start.5 = (bf16[16,1,32,2048]{3,2,1,0:T(8,128)(2,1)}, bf16[16,1,32,2048]{3,2,1,0:T(8,128)(2,1)S(1)}, u32[]{:S(2)}) copy-start(bf16[16,1,32,2048]{3,2,1,0:T(8,128)(2,1)S(1)} %get-tuple-element.9) | copy-start | bytes 6291460
  354.4 83.0 %all-to-all-start.3 = ((bf16[16,2,32,2048]{3,2,1,0:T(8,128)(2,1)}), bf16[16,2,32,2048]{3,2,1,0:T(8,128)(2,1)}, u32[]{:S(2)}, u32[]{:S(2)}) async-start(bf16[16,2,32,2048]{3,2,1,0:T(8,128)(2,1)} %pad_maximum_fusion), calls=%async_computation.4 | async-start | bytes 8388608 | tf_op jit(solution)/shard_map/all_to_all | solution.py:186
  359.7 120.0 %reduce-scatter.5.cloned.1.call-start = ((), (), s32[]{:S(2)}) async-start(), calls=%async_computation.9 | async-start | bytes 1572864 | tf_op jit(solution)/shard_map/reduce_scatter | solution.py:197
  437.4 44.1 %copy-start.1 = (f32[1024,64]{0,1:T(8,128)S(1)}, f32[1024,64]{0,1:T(8,128)}, u32[]{:S(2)}) copy-start(f32[1024,64]{0,1:T(8,128)} %param.28) | copy-start | bytes 786436
Sparse Core Ops, SparseCore 0:
  18.9 101.8 all-gather.2
  122.9 55.2 all-gather.4
  182.3 20.6 reduce-scatter.2
  444.4 35.2 reduce-scatter.4
where the time goes:
time: 494 us; the launch traced here: 488 us
  waiting for transfers between devices  241 us (49%)
  blocking collectives  123 us (25%)
  matrix products  54.4 us (11%)
  other arithmetic  25 us (5%)
  local copies, waits for them, and re-layouts  15.8 us (3%)
  starting transfers between devices  15.2 us (3%)
  between operations  13.8 us (3%)
    all_to_all x1, blocking collectives, local(): lax.all_to_all(sending.reshape(dp_count, held, CAP, D), 'dp', split_axis=...  98.4 us
    all_to_all x1, waiting for transfers between devices, local(): lax.all_to_all(jnp.stack(outs, axis=1), 'dp', split_axis=0, concat_axis=0...  77.5 us
    all_gather x1, waiting for transfers between devices, gather_tokens(): return lax.all_gather(block, 'dp', axis=0, tiled=True)  43.2 us
    all_to_all x1, waiting for transfers between devices, local(): lax.all_to_all(packed, 'dp', split_axis=0, concat_axis=0, tiled=True)  39.1 us
    reduce_scatter x1, waiting for transfers between devices, local(): mixture = lax.psum_scatter(mixture, 'mp', scatter_dimension=1, tiled=True)  35.4 us
    all_gather x1, waiting for transfers between devices, local(): all_output_weight = lax.all_gather(output_weight, 'dp', axis=1, tiled=True)  24.8 us
    dot_general x2, matrix products, local(): jnp.dot(hidden, down_local[low:high], preferred_element_type=jnp.float32)  20.5 us
    reduce_scatter x1, waiting for transfers between devices, local(): lax.psum_scatter(partial_out, 'mp', scatter_dimension=1, tiled=True)  20.2 us
  transfers between devices with their start and end apart: 7, of which 6 were waited for; matrix products, arithmetic and copies ran while one was open for 8% of the time, Pallas kernels for 0%

commit v1 on v0

--- a/solution.py
+++ b/solution.py
@@ -1,3 +1,4 @@
+import functools
 import jax
 import jax.numpy as jnp
 from jax import lax
@@ -14,6 +15,39 @@
 NEG = -1e30
 
 
+def solve_heaps(panel, dev_axis):
+    even = jax.lax.axis_size(dev_axis)
+    work_now, mixed_arr, frame_out = (even, jax.lax.axis_index(dev_axis), panel.shape[0])
+    row_out = kept_arr = panel
+    big = lax.dynamic_update_slice_in_dim(
+        jnp.zeros(
+            [dev_j * work_now if m == 0 else dev_j for m, dev_j in enumerate(panel.shape)],
+            panel.dtype,
+        ),
+        panel,
+        mixed_arr * frame_out,
+        axis=0,
+    )
+    for pp in range(1, work_now // 2 + 1):
+        row_out = jax.lax.ppermute(
+            row_out, dev_axis, [(m, (m + 1) % work_now) for m in range(work_now)]
+        )
+        big = lax.dynamic_update_slice_in_dim(
+            big, row_out, (mixed_arr - pp) % work_now * frame_out, axis=0
+        )
+        if 2 * pp < work_now:
+            kept_arr = jax.lax.ppermute(
+                kept_arr, dev_axis, [(m, (m - 1) % work_now) for m in range(work_now)]
+            )
+            big = lax.dynamic_update_slice_in_dim(
+                big, kept_arr, (mixed_arr + pp) % work_now * frame_out, axis=0
+            )
+    return big
+
+
+press_units = functools.partial(solve_heaps, dev_axis="dp")
+
+
 def rope_tables(position):
     halves = HEAD_DIM // 2
     exponent = jnp.arange(halves, dtype=jnp.float32) * (2.0 / HEAD_DIM)
@@ -46,7 +80,7 @@
 
 
 def gather_tokens(block):
-    return lax.all_gather(block, "dp", axis=0, tiled=True)
+    return press_units(block)
 
 
 def attention(queries, keys, values, query_seg, query_row, key_seg, key_row, keep_mask):

time: 494 us -> 527 us (1.067)
  waiting for transfers between devices: 241 us -> 205 us
  starting transfers between devices: 15.2 us -> 43.6 us
  local copies, waits for them, and re-layouts: 15.8 us -> 36.1 us
  blocking collectives: 123 us -> 142 us
    ppermute x0 -> x15, waiting for transfers between devices: none -> 73.2 us  [the longest x8 68.8 us: solve_heaps(): jax.lax.ppermute(row_out, dev_axis, [(m, (m + 1) % work_now) for m in ran...]
    all_gather x1 -> x0, waiting for transfers between devices: 43.2 us -> none  [gather_tokens(): return lax.all_gather(block, 'dp', axis=0, tiled=True)]
    all_to_all x1, waiting for transfers between devices: 39.1 us -> 0.01 us  [local(): lax.all_to_all(packed, 'dp', split_axis=0, concat_axis=0, tiled=True)]
    ppermute x0 -> x15, starting transfers between devices: none -> 33.7 us  [the longest x7 31.4 us: solve_heaps(): jax.lax.ppermute(kept_arr, dev_axis, [(m, (m - 1) % work_now) for m in ra...]
    all_gather x1, waiting for transfers between devices: 24.8 us -> 0.01 us  [local(): all_output_weight = lax.all_gather(output_weight, 'dp', axis=1, tiled=True)]
    all_to_all x0 -> x1, blocking collectives: none -> 19 us  [local(): lax.all_to_all(attended.reshape(local_heads, tok_rows, HEAD_DIM), 'dp', s...]
    dynamic_update_slice x0 -> x15, local copies, waits for them, and re-layouts: none -> 17.8 us  [the longest x8 9.88 us: solve_heaps(): lax.dynamic_update_slice_in_dim(big, row_out, (mixed_arr - pp) % work_now...]
  transfers between devices with their start and end apart: 7 -> 20, of which waited for: 6 -> 13; matrix products, arithmetic and copies ran while one was open for 8% -> 10% of each run, Pallas kernels for 0% -> 0%
where the time goes in v1:
time: 527 us; the launch traced here: 520 us
  waiting for transfers between devices  205 us (39%)
  blocking collectives  142 us (27%)
  matrix products  55.1 us (10%)
  starting transfers between devices  43.6 us (8%)
  local copies, waits for them, and re-layouts  36.1 us (7%)
  other arithmetic  23.8 us (5%)
  between operations  14.1 us (3%)
    all_to_all x1, blocking collectives, local(): lax.all_to_all(sending.reshape(dp_count, held, CAP, D), 'dp', split_axis=...  98.4 us
    all_to_all x1, waiting for transfers between devices, local(): lax.all_to_all(jnp.stack(outs, axis=1), 'dp', split_axis=0, concat_axis=0...  77.5 us
    ppermute x8, waiting for transfers between devices, solve_heaps(): jax.lax.ppermute(row_out, dev_axis, [(m, (m + 1) % work_now) for m in ran...  68.8 us
    reduce_scatter x1, waiting for transfers between devices, local(): mixture = lax.psum_scatter(mixture, 'mp', scatter_dimension=1, tiled=True)  35.4 us
    ppermute x7, starting transfers between devices, solve_heaps(): jax.lax.ppermute(kept_arr, dev_axis, [(m, (m - 1) % work_now) for m in ra...  31.4 us
    dot_general x2, matrix products, local(): jnp.dot(hidden, down_local[low:high], preferred_element_type=jnp.float32)  21.2 us
    all_to_all x1, blocking collectives, local(): lax.all_to_all(attended.reshape(local_heads, tok_rows, HEAD_DIM), 'dp', s...  19 us
    reduce_scatter x1, waiting for transfers between devices, local(): lax.psum_scatter(partial_out, 'mp', scatter_dimension=1, tiled=True)  18 us
  transfers between devices with their start and end apart: 20, of which 13 were waited for; matrix products, arithmetic and copies ran while one was open for 10% of the time, Pallas kernels for 0%

profile of v1, /device:TPU:0, one launch (start us, length us, event | category | flops | bytes accessed | tf_op | source)
XLA Modules:
  0.0 519.6 jit_solution(18368729937342853214)
XLA Ops:
  6.5 10.3 %all_gather.9 = bf16[128,2048]{1,0:T(8,128)(2,1)S(1)} all-gather(bf16[128,1024]{1,0:T(8,128)(2,1)} %param.16), channel_id=1, replica_groups=mesh['dp'=16,'mp'=2] {'mp'}, dimensions={1}, use_global_device_ids=true | all-gather | bytes 786432 | tf_op jit(solution)/shard_map/all_gather | solution.py:138
  22.4 4.4 collective-permute-start.1
  43.1 36.9 %collective-permute-done.2 = bf16[128,2048]{1,0:T(8,128)(2,1)} collective-permute-done((bf16[128,2048]{1,0:T(8,128)(2,1)S(1)}, bf16[128,2048]{1,0:T(8,128)(2,1)}, u32[]{:S(2)}, u32[]{:S(2)}) %collective-permute-start.2) | collective-permute-done | bytes 524320 | tf_op jit(solution)/shard_map/ppermute | solution.py:32
  83.8 4.5 collective-permute-start.5
  88.3 6.7 %collective-permute-done.4 = bf16[128,2048]{1,0:T(8,128)(2,1)} collective-permute-done((bf16[128,2048]{1,0:T(8,128)(2,1)}, bf16[128,2048]{1,0:T(8,128)(2,1)}, u32[]{:S(2)}, u32[]{:S(2)}) %collective-permute-start.4) | collective-permute-done | bytes 524320 | tf_op jit(solution)/shard_map/ppermute | solution.py:32
  98.8 4.6 collective-permute-start.7
  104.3 5.9 %collective-permute-done.6 = bf16[128,2048]{1,0:T(8,128)(2,1)} collective-permute-done((bf16[128,2048]{1,0:T(8,128)(2,1)}, bf16[128,2048]{1,0:T(8,128)(2,1)}, u32[]{:S(2)}, u32[]{:S(2)}) %collective-permute-start.6) | collective-permute-done | bytes 524320 | tf_op jit(solution)/shard_map/ppermute | solution.py:32
  120.3 7.1 %collective-permute-done.8 = bf16[128,2048]{1,0:T(8,128)(2,1)S(1)} collective-permute-done((bf16[128,2048]{1,0:T(8,128)(2,1)}, bf16[128,2048]{1,0:T(8,128)(2,1)S(1)}, u32[]{:S(2)}, u32[]{:S(2)}) %collective-permute-start.8) | collective-permute-done | bytes 524320 | tf_op jit(solution)/shard_map/ppermute | solution.py:32
  131.3 4.4 collective-permute-start.11
  142.4 4.7 collective-permute-start.13
  154.6 7.4 %collective-permute-done.14 = bf16[128,2048]{1,0:T(8,128)(2,1)S(1)} collective-permute-done((bf16[128,2048]{1,0:T(8,128)(2,1)S(1)}, bf16[128,2048]{1,0:T(8,128)(2,1)S(1)}, u32[]{:S(2)}, u32[]{:S(2)}) %collective-permute-start.14) | collective-permute-done | bytes 524320 | tf_op jit(solution)/shard_map/ppermute | solution.py:32
  162.9 6.4 %fusion.89 = f32[2048,384]{0,1:T(8,128)S(1)} fusion(bf16[2048,2048]{1,0:T(8,128)(2,1)} %constant_dynamic-update-slice_fusion, bf16[2048,384]{1,0:T(8,128)(2,1)} %bitcast.11), kind=kOutput, calls=%fused_computation.146 | convolution fusion | flops 3221225472 | bytes 13107200 | tf_op jit(solution)/shard_map/dot_general | solution.py:154
  182.2 5.0 fusion.3
  191.3 19.0 %all_to_all.20 = bf16[8,128,128]{1,2,0:T(8,128)(2,1)S(1)} all-to-all(bf16[8,128,128]{1,2,0:T(8,128)(2,1)S(1)} %copy.45), channel_id=1, replica_groups={{0,4,8,12,16,20,24,28},{2,6,10,14,18,22,26,30},{1,5,9,13,17,21,25,29},{..., dimensions={0} | all-to-all | bytes 524288 | tf_op jit(solution)/shard_map/all_to_all | solution.py:162
  214.8 18.0 %reduce-scatter.3.cloned.1.call-done = f32[128,1024]{1,0:T(8,128)} async-done(((f32[128,2048]{1,0:T(8,128)}), f32[128,1024]{1,0:T(8,128)}) %reduce-scatter.3.cloned.1.call-update) | async-done | bytes 524304 | tf_op jit(solution)/shard_map/reduce_scatter | solution.py:172
  234.7 7.3 %all-reduce = (f32[128]{0:T(128)S(1)}, f32[128,64]{0,1:T(8,128)S(1)}) all-reduce(f32[128]{0:T(128)S(1)} %get-tuple-element.7, f32[128,64]{0,1:T(8,128)S(1)} %fusion.50), channel_id=1, replica_groups=mesh['dp'=16,'mp'=2] {'mp'}, use_global_device_ids=true, to_apply=%region_12.13 | all-reduce | flops 8320 | bytes 66560 | tf_op jit(solution)/shard_map/psum | solution.py:177
  242.1 7.0 %all_gather.11 = bf16[128,2048]{1,0:T(8,128)(2,1)S(1)} all-gather(bf16[128,1024]{1,0:T(8,128)(2,1)S(1)} %fusion.51), channel_id=1, replica_groups=mesh['dp'=16,'mp'=2] {'mp'}, dimensions={1}, use_global_device_ids=true | all-gather | bytes 786432 | tf_op jit(solution)/shard_map/all_gather | solution.py:206
  250.4 98.4 %all_to_all.21 = bf16[16,2,32,2048]{3,2,1,0:T(8,128)(2,1)S(1)} all-to-all(bf16[16,2,32,2048]{3,2,1,0:T(8,128)(2,1)S(1)} %bitcast.92), channel_id=1, replica_groups=mesh['dp'=16,'mp'=2] {'dp'}, dimensions={0} | all-to-all | bytes 8388608 | tf_op jit(solution)/shard_map/all_to_all | solution.py:208
  359.9 10.6 %fusion.21 = bf16[512,2048]{1,0:T(8,128)(2,1)} fusion(bf16[1,2048,2048]{2,1,0:T(8,128)(2,1)} %param.31, f32[512,1024]{1,0:T(8,128)} %fusion.11, bf16[512,2048]{1,0:T(8,128)(2,1)} %bitcast.99, bf16[2048,2048]{1,0:T(8,128)(2,1)} %bitcast.123), kind=kOutput, calls=%fused_computation.25 | convolution fusion | flops 4299161600 | bytes 14680064 | tf_op jit(solution)/shard_map/dot_general | solution.py:218
  370.5 10.6 %fusion.24 = bf16[512,2048]{1,0:T(8,128)(2,1)} fusion(bf16[1,2048,2048]{2,1,0:T(8,128)(2,1)} %param.31, f32[512,1024]{1,0:T(8,128)} %fusion.7, bf16[512,2048]{1,0:T(8,128)(2,1)} %bitcast.97, bf16[2048,2048]{1,0:T(8,128)(2,1)} %bitcast.124), kind=kOutput, calls=%fused_computation.26 | convolution fusion | flops 4299161600 | bytes 14680064 | tf_op jit(solution)/shard_map/dot_general | solution.py:218
  381.1 4.6 pad_maximum_fusion
  385.7 5.3 %all-to-all-start.3 = ((bf16[16,2,32,2048]{3,2,1,0:T(8,128)(2,1)}), bf16[16,2,32,2048]{3,2,1,0:T(8,128)(2,1)}, u32[]{:S(2)}, u32[]{:S(2)}) async-start(bf16[16,2,32,2048]{3,2,1,0:T(8,128)(2,1)} %pad_maximum_fusion), calls=%async_computation.4 | async-start | bytes 8388608 | tf_op jit(solution)/shard_map/all_to_all | solution.py:220
  391.1 77.5 %all-to-all-done.3 = bf16[16,2,32,2048]{3,2,1,0:T(8,128)(2,1)} async-done(((bf16[16,2,32,2048]{3,2,1,0:T(8,128)(2,1)}), bf16[16,2,32,2048]{3,2,1,0:T(8,128)(2,1)}, u32[]{:S(2)}, u32[]{:S(2)}) %all-to-all-start.3) | async-done | bytes 4194336 | tf_op jit(solution)/shard_map/all_to_all | solution.py:220
  475.6 35.4 %reduce-scatter.5.cloned.1.call-done = f32[128,1024]{1,0:T(8,128)} async-done(((f32[128,2048]{1,0:T(8,128)}), f32[128,1024]{1,0:T(8,128)}) %reduce-scatter.5.cloned.1.call-update) | async-done | bytes 524304 | tf_op jit(solution)/shard_map/reduce_scatter | solution.py:231
  (146 shorter events, 103.2 us)
Async XLA Ops:
  6.5 227.5 %copy-start = (f32[1024,64]{0,1:T(8,128)S(1)}, f32[1024,64]{0,1:T(8,128)}, u32[]{:S(2)}) copy-start(f32[1024,64]{0,1:T(8,128)} %param.28) | copy-start | bytes 786436
  22.4 13.4 %collective-permute-start = (bf16[128,2048]{1,0:T(8,128)(2,1)S(1)}, bf16[128,2048]{1,0:T(8,128)(2,1)S(1)}, u32[]{:S(2)}, u32[]{:S(2)}) collective-permute-start(bf16[128,2048]{1,0:T(8,128)(2,1)S(1)} %get-tuple-element.10), channel_id=1, source_target_pairs={{0,2},{2,4},{4,6},{6,8},{8,10},{10,12},{12,14},{14,16},{16,18},{18... | collective-permute-start | bytes 1572872 | tf_op jit(solution)/shard_map/ppermute | solution.py:32
  22.4 13.7 %collective-permute-start.1 = (bf16[128,2048]{1,0:T(8,128)(2,1)S(1)}, bf16[128,2048]{1,0:T(8,128)(2,1)S(1)}, u32[]{:S(2)}, u32[]{:S(2)}) collective-permute-start(bf16[128,2048]{1,0:T(8,128)(2,1)S(1)} %get-tuple-element.10), channel_id=1, source_target_pairs={{0,30},{2,0},{4,2},{6,4},{8,6},{10,8},{12,10},{14,12},{16,14},{18,... | collective-permute-start | bytes 1572872 | tf_op jit(solution)/shard_map/ppermute | solution.py:39
  28.8 59.5 %copy-start.14 = (s32[2048]{0:T(1024)S(1)}, s32[2048]{0:T(1024)}, u32[]{:S(2)}) copy-start(s32[2048]{0:T(1024)} %param.18) | copy-start | bytes 24580
  30.1 132.7 %all-to-all-start = ((bf16[16,128,384]{2,1,0:T(8,128)(2,1)}), bf16[16,128,384]{2,1,0:T(8,128)(2,1)}, u32[]{:S(2)}, u32[]{:S(2)}) async-start(bf16[16,128,384]{2,1,0:T(8,128)(2,1)} %bitcast.10), calls=%async_computation | async-start | bytes 3145728 | tf_op jit(solution)/shard_map/all_to_all | solution.py:136
  34.6 175.7 %all-gather.2.cloned.1.call-start = ((), (), s32[]{:S(2)}) async-start(), calls=%async_computation.6 | async-start | bytes 4456448 | tf_op jit(solution)/shard_map/all_gather | solution.py:144
  35.3 197.5 %reduce-scatter.3.cloned.1.call-start = ((), (), s32[]{:S(2)}) async-start(), calls=%async_computation.7 | async-start | bytes 1572864 | tf_op jit(solution)/shard_map/reduce_scatter | solution.py:172
  35.8 44.3 %collective-permute-start.2 = (bf16[128,2048]{1,0:T(8,128)(2,1)S(1)}, bf16[128,2048]{1,0:T(8,128)(2,1)}, u32[]{:S(2)}, u32[]{:S(2)}) collective-permute-start(bf16[128,2048]{1,0:T(8,128)(2,1)S(1)} %collective-permute-done), channel_id=1, source_target_pairs={{0,2},{2,4},{4,6},{6,8},{8,10},{10,12},{12,14},{14,16},{16,18},{18... | collective-permute-start | bytes 1572872 | tf_op jit(solution)/shard_map/ppermute | solution.py:32
  36.1 47.7 %collective-permute-start.3 = (bf16[128,2048]{1,0:T(8,128)(2,1)S(1)}, bf16[128,2048]{1,0:T(8,128)(2,1)}, u32[]{:S(2)}, u32[]{:S(2)}) collective-permute-start(bf16[128,2048]{1,0:T(8,128)(2,1)S(1)} %collective-permute-done.1), channel_id=1, source_target_pairs={{0,30},{2,0},{4,2},{6,4},{8,6},{10,8},{12,10},{14,12},{16,14},{18,... | collective-permute-start | bytes 1572872 | tf_op jit(solution)/shard_map/ppermute | solution.py:39
  80.0 14.9 %collective-permute-start.4 = (bf16[128,2048]{1,0:T(8,128)(2,1)}, bf16[128,2048]{1,0:T(8,128)(2,1)}, u32[]{:S(2)}, u32[]{:S(2)}) collective-permute-start(bf16[128,2048]{1,0:T(8,128)(2,1)} %collective-permute-done.2), channel_id=1, source_target_pairs={{0,2},{2,4},{4,6},{6,8},{8,10},{10,12},{12,14},{14,16},{16,18},{18... | collective-permute-start | bytes 1572872 | tf_op jit(solution)/shard_map/ppermute | solution.py:32
  83.8 15.1 %collective-permute-start.5 = (bf16[128,2048]{1,0:T(8,128)(2,1)}, bf16[128,2048]{1,0:T(8,128)(2,1)}, u32[]{:S(2)}, u32[]{:S(2)}) collective-permute-start(bf16[128,2048]{1,0:T(8,128)(2,1)} %collective-permute-done.3), channel_id=1, source_target_pairs={{0,30},{2,0},{4,2},{6,4},{8,6},{10,8},{12,10},{14,12},{16,14},{18,... | collective-permute-start | bytes 1572872 | tf_op jit(solution)/shard_map/ppermute | solution.py:39
  95.0 15.2 %collective-permute-start.6 = (bf16[128,2048]{1,0:T(8,128)(2,1)}, bf16[128,2048]{1,0:T(8,128)(2,1)}, u32[]{:S(2)}, u32[]{:S(2)}) collective-permute-start(bf16[128,2048]{1,0:T(8,128)(2,1)} %collective-permute-done.4), channel_id=1, source_target_pairs={{0,2},{2,4},{4,6},{6,8},{8,10},{10,12},{12,14},{14,16},{16,18},{18... | collective-permute-start | bytes 1572872 | tf_op jit(solution)/shard_map/ppermute | solution.py:32
  98.8 15.2 %collective-permute-start.7 = (bf16[128,2048]{1,0:T(8,128)(2,1)}, bf16[128,2048]{1,0:T(8,128)(2,1)S(1)}, u32[]{:S(2)}, u32[]{:S(2)}) collective-permute-start(bf16[128,2048]{1,0:T(8,128)(2,1)} %collective-permute-done.5), channel_id=1, source_target_pairs={{0,30},{2,0},{4,2},{6,4},{8,6},{10,8},{12,10},{14,12},{16,14},{18,... | collective-permute-start | bytes 1572872 | tf_op jit(solution)/shard_map/ppermute | solution.py:39
  110.2 17.2 %collective-permute-start.8 = (bf16[128,2048]{1,0:T(8,128)(2,1)}, bf16[128,2048]{1,0:T(8,128)(2,1)S(1)}, u32[]{:S(2)}, u32[]{:S(2)}) collective-permute-start(bf16[128,2048]{1,0:T(8,128)(2,1)} %collective-permute-done.6), channel_id=1, source_target_pairs={{0,2},{2,4},{4,6},{6,8},{8,10},{10,12},{12,14},{14,16},{16,18},{18... | collective-permute-start | bytes 1572872 | tf_op jit(solution)/shard_map/ppermute | solution.py:32
  114.0 17.2 %collective-permute-start.9 = (bf16[128,2048]{1,0:T(8,128)(2,1)S(1)}, bf16[128,2048]{1,0:T(8,128)(2,1)S(1)}, u32[]{:S(2)}, u32[]{:S(2)}) collective-permute-start(bf16[128,2048]{1,0:T(8,128)(2,1)S(1)} %collective-permute-done.7), channel_id=1, source_target_pairs={{0,30},{2,0},{4,2},{6,4},{8,6},{10,8},{12,10},{14,12},{16,14},{18,... | collective-permute-start | bytes 1572872 | tf_op jit(solution)/shard_map/ppermute | solution.py:39
  127.5 11.4 %collective-permute-start.10 = (bf16[128,2048]{1,0:T(8,128)(2,1)S(1)}, bf16[128,2048]{1,0:T(8,128)(2,1)S(1)}, u32[]{:S(2)}, u32[]{:S(2)}) collective-permute-start(bf16[128,2048]{1,0:T(8,128)(2,1)S(1)} %collective-permute-done.8), channel_id=1, source_target_pairs={{0,2},{2,4},{4,6},{6,8},{8,10},{10,12},{12,14},{14,16},{16,18},{18... | collective-permute-start | bytes 1572872 | tf_op jit(solution)/shard_map/ppermute | solution.py:32
  131.3 11.1 %collective-permute-start.11 = (bf16[128,2048]{1,0:T(8,128)(2,1)S(1)}, bf16[128,2048]{1,0:T(8,128)(2,1)S(1)}, u32[]{:S(2)}, u32[]{:S(2)}) collective-permute-start(bf16[128,2048]{1,0:T(8,128)(2,1)S(1)} %collective-permute-done.9), channel_id=1, source_target_pairs={{0,30},{2,0},{4,2},{6,4},{8,6},{10,8},{12,10},{14,12},{16,14},{18,... | collective-permute-start | bytes 1572872 | tf_op jit(solution)/shard_map/ppermute | solution.py:39
  138.9 11.4 %collective-permute-start.12 = (bf16[128,2048]{1,0:T(8,128)(2,1)S(1)}, bf16[128,2048]{1,0:T(8,128)(2,1)S(1)}, u32[]{:S(2)}, u32[]{:S(2)}) collective-permute-start(bf16[128,2048]{1,0:T(8,128)(2,1)S(1)} %collective-permute-done.10), channel_id=1, source_target_pairs={{0,2},{2,4},{4,6},{6,8},{8,10},{10,12},{12,14},{14,16},{16,18},{18... | collective-permute-start | bytes 1572872 | tf_op jit(solution)/shard_map/ppermute | solution.py:32
  142.4 11.4 %collective-permute-start.13 = (bf16[128,2048]{1,0:T(8,128)(2,1)S(1)}, bf16[128,2048]{1,0:T(8,128)(2,1)S(1)}, u32[]{:S(2)}, u32[]{:S(2)}) collective-permute-start(bf16[128,2048]{1,0:T(8,128)(2,1)S(1)} %collective-permute-done.11), channel_id=1, source_target_pairs={{0,30},{2,0},{4,2},{6,4},{8,6},{10,8},{12,10},{14,12},{16,14},{18,... | collective-permute-start | bytes 1572872 | tf_op jit(solution)/shard_map/ppermute | solution.py:39
  150.3 11.7 %collective-permute-start.14 = (bf16[128,2048]{1,0:T(8,128)(2,1)S(1)}, bf16[128,2048]{1,0:T(8,128)(2,1)S(1)}, u32[]{:S(2)}, u32[]{:S(2)}) collective-permute-start(bf16[128,2048]{1,0:T(8,128)(2,1)S(1)} %collective-permute-done.12), channel_id=1, source_target_pairs={{0,2},{2,4},{4,6},{6,8},{8,10},{10,12},{12,14},{14,16},{16,18},{18... | collective-permute-start | bytes 1572872 | tf_op jit(solution)/shard_map/ppermute | solution.py:32
  250.4 99.0 %slice-start = ((s8[8388608]{0:T(1024)(128)(4,1)}), s8[4194304]{0:T(1024)(128)(4,1)S(1)}, s32[]{:S(2)}) async-start(s8[8388608]{0:T(1024)(128)(4,1)} %bitcast.119), calls=%async_computation.9 | async-start | bytes 8388608
  385.7 83.0 %all-to-all-start.3 = ((bf16[16,2,32,2048]{3,2,1,0:T(8,128)(2,1)}), bf16[16,2,32,2048]{3,2,1,0:T(8,128)(2,1)}, u32[]{:S(2)}, u32[]{:S(2)}) async-start(bf16[16,2,32,2048]{3,2,1,0:T(8,128)(2,1)} %pad_maximum_fusion), calls=%async_computation.4 | async-start | bytes 8388608 | tf_op jit(solution)/shard_map/all_to_all | solution.py:220
  391.0 120.1 %reduce-scatter.5.cloned.1.call-start = ((), (), s32[]{:S(2)}) async-start(), calls=%async_computation.8 | async-start | bytes 1572864 | tf_op jit(solution)/shard_map/reduce_scatter | solution.py:231
  468.7 44.2 %copy-start.1 = (f32[1024,64]{0,1:T(8,128)S(1)}, f32[1024,64]{0,1:T(8,128)}, u32[]{:S(2)}) copy-start(f32[1024,64]{0,1:T(8,128)} %param.28) | copy-start | bytes 786436
  (17 other events, 179.1 us)
Sparse Core Ops, SparseCore 0:
  37.6 86.9 all-gather.1
  214.3 18.4 reduce-scatter.2
  475.7 35.2 reduce-scatter.4
